TPU v7x, 512 devices: a whole 4x4x16 slice. The times are simulated.
512 devices in a mesh: dp: 128 (over z, x, core), mp: 4 (over y).
Axes of the slice: x: 4, y: 4, z: 16, core: 2. Of those that a mesh axis runs over, the one named last changes fastest.
Arguments:
- session_length: int32 [128], P('dp'), may hold values from 1 to 128
- event_owner: int32 [16384, 1], P('dp'), may hold values from 0 to 127; in each aligned block of 128 rows (0 to 127, 128 to 255, ...) at most 2 rows name the same one
- event_row: int32 [16384], P('dp'), may hold values from 0 to 255
- text_rows: bfloat16 [32768, 4096], P('dp', 'mp'), may hold values from -6 to 6
- image_rows: bfloat16 [32768, 4096], P('dp', 'mp'), may hold values from -6 to 6
- price: float32 [32768], P('dp'), may hold values from 0.2 to 5
- price_dir: bfloat16 [4096], P('mp'), may hold values from -4 to 4
- norm_gain: bfloat16 [4096], P('mp'), may hold values from 0.5 to 1.5
- w_query: bfloat16 [4096, 2048], P('dp', 'mp'), may hold values from -1 to 1
- w_key: bfloat16 [4096, 2048], P('dp', 'mp'), may hold values from -1 to 1
- w_value: bfloat16 [4096, 2048], P('dp', 'mp'), may hold values from -0.09375 to 0.09375
- cotangent: bfloat16 [16384, 4096], P('dp', 'mp'), may hold values from -6 to 6
Outputs:
- context: bfloat16 [16384, 2048], P('dp', 'mp')
- text_grad: float32 [32768, 4096], P('dp', 'mp')
- image_grad: float32 [32768, 4096], P('dp', 'mp')
Inputs may be any that keep to these rules, and one draw needn't show every extreme that they name: `event_owner`: among the event slots of one index of dp, no owner is named more than 2 times, a bound that some block reaches.
All inputs are finite; a program needn't handle non-finite values.
Results may differ from a plain program's by a relative error of at most 0.0063.
Values may be sent and summed in bfloat16 or wider, within the bound.
No kernel may reach another device: no remote copies, remote signals or barrier semaphores. Data moves between devices by JAX's collectives and lax.ppermute only.
A program may use at most 64 MiB of HBM per device.

v0:
```python
import math
import jax
import jax.numpy as jnp
from jax import lax
from jax.sharding import PartitionSpec as P

HD = 128
SLOT = 128


def one_hot(rows, columns):
    return (rows[:, None] == columns[None, :]).astype(jnp.bfloat16)


def pick(selector, values):
    return jnp.dot(selector, values, preferred_element_type=jnp.float32)


def attend(query, keys, values, session_length):
    heads_here = query.shape[1] // HD
    shape3 = (SLOT, heads_here, HD)
    scores = jnp.einsum(
        "qhd,khd->hqk",
        query.reshape(shape3),
        keys.reshape(shape3),
        preferred_element_type=jnp.float32,
    ) / math.sqrt(HD)
    position = jnp.arange(SLOT, dtype=jnp.int32)
    live_mask = position < session_length[0]
    allowed = (position[None, :] <= position[:, None])[None] & live_mask[None, None, :]
    scores = jnp.where(allowed, scores, jnp.float32(-1e30))
    row_max = jnp.max(scores, axis=-1, keepdims=True)
    powers = jnp.exp(scores - row_max)
    probs = (powers / jnp.sum(powers, axis=-1, keepdims=True)).astype(jnp.bfloat16)
    context = jnp.einsum(
        "hqk,khd->qhd", probs, values.reshape(shape3), preferred_element_type=jnp.float32
    )
    context = jnp.where(live_mask[:, None, None], context, jnp.float32(0.0))
    return context.reshape(SLOT, heads_here * HD).astype(jnp.bfloat16)


def local(
    session_length,
    event_owner,
    event_row,
    text_rows,
    image_rows,
    price,
    price_dir,
    norm_gain,
    w_query,
    w_key,
    w_value,
    cotangent,
):
    peers = lax.axis_size("dp")
    parts = lax.axis_size("mp")
    mine = lax.axis_index("mp")
    tok_count = event_row.shape[0]
    capacity = 2 * tok_count // peers
    col_width = text_rows.shape[1]
    table_rows = text_rows.shape[0]
    slots = jnp.arange(peers * capacity, dtype=jnp.int32)
    weights = lax.all_gather(
        jnp.concatenate([w_query, w_key, w_value], axis=1), "dp", axis=0, tiled=True
    )
    owner_ids = event_owner[:, 0]
    place = jnp.arange(tok_count, dtype=jnp.int32)
    same = (owner_ids[:, None] == owner_ids[None, :]) & (place[None, :] < place[:, None])
    slot_ids = owner_ids * capacity + jnp.sum(same.astype(jnp.int32), axis=1)
    taken = slots[:, None] == slot_ids[None, :]
    requests = (jnp.sum(jnp.where(taken, event_row[None, :] + 1, 0), axis=1) - 1).reshape(
        peers, capacity
    )
    got_ids = lax.all_to_all(requests, "dp", split_axis=0, concat_axis=0, tiled=True).reshape(-1)
    text_float = text_rows.astype(jnp.float32)
    image_float = image_rows.astype(jnp.float32)
    table = (
        text_float * image_float + price[:, None] * price_dir.astype(jnp.float32)[None, :]
    ).astype(jnp.bfloat16)
    wanted = one_hot(got_ids, jnp.arange(table_rows, dtype=jnp.int32))
    replies = lax.all_to_all(
        pick(wanted, table).astype(jnp.bfloat16).reshape(peers, capacity, col_width),
        "dp",
        split_axis=0,
        concat_axis=0,
        tiled=True,
    ).reshape(peers * capacity, col_width)
    grad_buffer = pick(taken.astype(jnp.bfloat16), cotangent).astype(jnp.bfloat16)
    grad_buffer, replies = lax.optimization_barrier((grad_buffer, replies))
    got_grads = lax.all_to_all(
        grad_buffer.reshape(peers, capacity, col_width),
        "dp",
        split_axis=0,
        concat_axis=0,
        tiled=True,
    ).reshape(peers * capacity, col_width)
    row_sums = pick(wanted.T, got_grads)
    text_grad = row_sums * image_float
    image_grad = row_sums * text_float
    joined = pick(one_hot(slot_ids, slots), replies).astype(jnp.bfloat16)
    turns = [
        (
            joined
            if k == 0
            else lax.ppermute(joined, "mp", [(i, (i + k) % parts) for i in range(parts)])
        )
        for k in range(parts)
    ]
    stacked = jnp.stack(turns)
    features = jnp.concatenate(
        [
            lax.dynamic_index_in_dim(stacked, (mine - s) % parts, 0, keepdims=False)
            for s in range(parts)
        ],
        axis=1,
    ).astype(jnp.float32)
    gain = lax.all_gather(norm_gain, "mp", axis=0, tiled=True).astype(jnp.float32)
    scale = lax.rsqrt(jnp.mean(features * features, axis=1, keepdims=True) + 1e-06)
    normed = (features * scale * gain[None, :]).astype(jnp.bfloat16)
    projected = jnp.dot(normed, weights, preferred_element_type=jnp.float32).astype(jnp.bfloat16)
    width = w_query.shape[1]
    context = attend(
        projected[:, :width],
        projected[:, width : 2 * width],
        projected[:, 2 * width :],
        session_length,
    )
    return (context, text_grad, image_grad)


def solution(mesh):
    return jax.shard_map(
        local,
        mesh=mesh,
        in_specs=(
            P("dp"),
            P("dp", None),
            P("dp"),
            P("dp", "mp"),
            P("dp", "mp"),
            P("dp"),
            P("mp"),
            P("mp"),
            P("dp", "mp"),
            P("dp", "mp"),
            P("dp", "mp"),
            P("dp", "mp"),
        ),
        out_specs=(P("dp", "mp"), P("dp", "mp"), P("dp", "mp")),
        check_vma=False,
    )
```

profile of v0, /device:TPU:1, one launch (start us, length us, event | category | flops | bytes accessed | tf_op | source)
XLA Modules:
  0.0 196.3 jit_solution(1731019495664114980)
XLA Ops:
  7.2 0.0 copy-start
  7.2 0.0 all-gather.2.cloned.1.call-start
  7.2 1.5 pad_maximum_fusion.3
  8.7 0.0 all-gather.2.cloned.1.call-update
  8.7 0.9 convert_reduce_fusion
  9.6 0.7 multiply_add_fusion
  10.3 0.1 select_reduce_fusion
  10.4 0.8 sub.24
  11.2 20.4 %all-to-all-start = ((s32[128,1,2]{2,1,0:T(1,128)}), s32[128,1,2]{2,1,0:T(1,128)S(1)}, u32[]{:S(2)}, u32[]{:S(2)}) async-start(s32[128,1,2]{2,1,0:T(1,128)} %bitcast.4), calls=%async_computation | async-start | bytes 131072 | tf_op jit(solution)/shard_map/all_to_all | solution.py:75
  31.6 0.7 convert_element_type.55
  32.3 14.1 %all-to-all-done = s32[128,1,2]{2,1,0:T(1,128)S(1)} async-done(((s32[128,1,2]{2,1,0:T(1,128)}), s32[128,1,2]{2,1,0:T(1,128)S(1)}, u32[]{:S(2)}, u32[]{:S(2)}) %all-to-all-start) | async-done | bytes 1056 | tf_op jit(solution)/shard_map/all_to_all | solution.py:75
  46.4 0.5 broadcast.75
  47.0 0.8 reduce.3
  47.8 0.1 eq.74
  47.9 1.7 convolution_convert_fusion.1
  49.6 1.0 reshape.110
  50.6 5.7 %all-to-all-start.1 = ((bf16[128,2,1024]{2,1,0:T(2,128)(2,1)}), bf16[128,2,1024]{2,1,0:T(2,128)(2,1)S(1)}, u32[]{:S(2)}, u32[]{:S(2)}) async-start(bf16[128,2,1024]{2,1,0:T(2,128)(2,1)} %reshape.110), calls=%async_computation.1 | async-start | bytes 1048576 | tf_op jit(solution)/shard_map/all_to_all | solution.py:82
  56.3 0.0 copy-done
  56.3 0.0 copy-start.4
  56.3 0.3 convolution_convert_fusion.2
  56.6 0.0 copy-start.3
  56.6 33.6 %all-to-all-done.1 = bf16[128,2,1024]{2,1,0:T(2,128)(2,1)S(1)} async-done(((bf16[128,2,1024]{2,1,0:T(2,128)(2,1)}), bf16[128,2,1024]{2,1,0:T(2,128)(2,1)S(1)}, u32[]{:S(2)}, u32[]{:S(2)}) %all-to-all-start.1) | async-done | bytes 524320 | tf_op jit(solution)/shard_map/all_to_all | solution.py:82
  90.2 0.2 reshape.111
  90.4 1.0 reshape.115
  91.3 9.5 %all-to-all-start.2 = ((bf16[128,2,1024]{2,1,0:T(2,128)(2,1)}), bf16[128,2,1024]{2,1,0:T(2,128)(2,1)S(1)}, u32[]{:S(2)}, u32[]{:S(2)}) async-start(bf16[128,2,1024]{2,1,0:T(2,128)(2,1)} %reshape.115), calls=%async_computation.2 | async-start | bytes 1048576 | tf_op jit(solution)/shard_map/all_to_all | solution.py:91
  101.5 0.0 copy-done.4
  101.6 0.3 convolution_convert_fusion.3
  101.8 3.2 %collective-permute-start = (bf16[128,1024]{1,0:T(8,128)(2,1)S(1)}, bf16[128,1024]{1,0:T(8,128)(2,1)S(1)}, u32[]{:S(2)}, u32[]{:S(2)}) collective-permute-start(bf16[128,1024]{1,0:T(8,128)(2,1)S(1)} %convolution_convert_fusion.3), channel_id=1, source_target_pairs={{0,1},{1,2},{2,3},{3,0},{4,5},{5,6},{6,7},{7,4},{8,9},{9,10},{10,1... | collective-permute-start | bytes 786440 | tf_op jit(solution)/shard_map/ppermute | solution.py:106
  105.0 4.4 %collective-permute-start.1 = (bf16[128,1024]{1,0:T(8,128)(2,1)S(1)}, bf16[128,1024]{1,0:T(8,128)(2,1)S(1)}, u32[]{:S(2)}, u32[]{:S(2)}) collective-permute-start(bf16[128,1024]{1,0:T(8,128)(2,1)S(1)} %convolution_convert_fusion.3), channel_id=1, source_target_pairs={{0,2},{1,3},{2,0},{3,1},{4,6},{5,7},{6,4},{7,5},{8,10},{9,11},{10,... | collective-permute-start | bytes 786440 | tf_op jit(solution)/shard_map/ppermute | solution.py:106
  109.4 3.0 %collective-permute-start.2 = (bf16[128,1024]{1,0:T(8,128)(2,1)S(1)}, bf16[128,1024]{1,0:T(8,128)(2,1)S(1)}, u32[]{:S(2)}, u32[]{:S(2)}) collective-permute-start(bf16[128,1024]{1,0:T(8,128)(2,1)S(1)} %convolution_convert_fusion.3), channel_id=1, source_target_pairs={{0,3},{1,0},{2,1},{3,2},{4,7},{5,4},{6,5},{7,6},{8,11},{9,8},{10,9... | collective-permute-start | bytes 786440 | tf_op jit(solution)/shard_map/ppermute | solution.py:106
  112.5 0.0 copy-done.3
  112.5 13.0 %all_gather.6 = bf16[4096]{0:T(1024)(128)(2,1)S(1)} all-gather(bf16[1024]{0:T(1024)(128)(2,1)S(1)} %copy-done.3), channel_id=1, replica_groups=mesh['dp'=128,'mp'=4] {'mp'}, dimensions={0}, use_global_device_ids=true | all-gather | bytes 10240 | tf_op jit(solution)/shard_map/all_gather | solution.py:118
  125.6 0.1 fusion.27
  125.7 0.0 collective-permute-done
  125.7 0.0 collective-permute-done.1
  125.7 0.0 collective-permute-done.2
  125.7 0.1 pad_maximum_fusion
  125.9 0.0 copy-start.1
  125.9 0.0 copy-start.2
  125.9 0.1 dynamic-slice_bitcast_fusion.3
  126.0 0.3 fusion.1
  126.3 7.7 %all-to-all-done.2 = bf16[128,2,1024]{2,1,0:T(2,128)(2,1)S(1)} async-done(((bf16[128,2,1024]{2,1,0:T(2,128)(2,1)}), bf16[128,2,1024]{2,1,0:T(2,128)(2,1)S(1)}, u32[]{:S(2)}, u32[]{:S(2)}) %all-to-all-start.2) | async-done | bytes 524320 | tf_op jit(solution)/shard_map/all_to_all | solution.py:91
  134.0 0.2 reshape.116
  134.2 0.0 copy-done.1
  134.2 0.0 copy-done.2
  134.3 1.7 convert_multiply_fusion.4
  136.0 45.6 %all-gather.2.cloned.1.call-done = bf16[4096,1536]{1,0:T(8,128)(2,1)} async-done(((bf16[32,1536]{1,0:T(8,128)(2,1)}), bf16[4096,1536]{1,0:T(8,128)(2,1)}) %all-gather.2.cloned.1.call-update) | async-done | bytes 12582928 | tf_op jit(solution)/shard_map/all_gather | solution.py:64
  181.6 6.4 %convolution_convert_fusion = bf16[128,1536]{1,0:T(8,128)(2,1)S(1)} fusion(bf16[4096,1536]{1,0:T(8,128)(2,1)} %all-gather.2.cloned.1.call-done, f32[4096]{0:T(1024)S(1)} %convert_element_type.60, f32[128]{0:T(128)S(1)} %add_rsqrt_fusion, bf16[128,1024]{1,0:T(8,128)(2,1)S(1)} %get-tuple-element.22, bf16[128,1024]{1,0:T(8,128)(2,1)S(1)} %get-tuple-element.23, ...), kind=kOutput, calls=%fused_computation.3 | convolution fusion | flops 1616576512 | bytes 14041600 | tf_op jit(solution)/shard_map/dot_general | solution.py:121
  188.0 0.2 fusion.5
  188.2 0.1 fusion.31
  188.3 0.1 copy.38
  188.4 0.2 fusion.7
  188.7 0.8 copy.36
  (6 shorter events, 0.1 us)
Async XLA Ops:
  7.2 49.1 %copy-start = (bf16[128,1024]{1,0:T(8,128)(2,1)S(1)}, bf16[128,1024]{1,0:T(8,128)(2,1)}, u32[]{:S(2)}) copy-start(bf16[128,1024]{1,0:T(8,128)(2,1)} %param.23) | copy-start | bytes 786436
  7.2 174.4 %all-gather.2.cloned.1.call-start = ((), (), s32[]{:S(2)}) async-start(), calls=%async_computation.3 | async-start | bytes 12681216 | tf_op jit(solution)/shard_map/all_gather | solution.py:64
  11.2 35.2 %all-to-all-start = ((s32[128,1,2]{2,1,0:T(1,128)}), s32[128,1,2]{2,1,0:T(1,128)S(1)}, u32[]{:S(2)}, u32[]{:S(2)}) async-start(s32[128,1,2]{2,1,0:T(1,128)} %bitcast.4), calls=%async_computation | async-start | bytes 131072 | tf_op jit(solution)/shard_map/all_to_all | solution.py:75
  50.6 39.6 %all-to-all-start.1 = ((bf16[128,2,1024]{2,1,0:T(2,128)(2,1)}), bf16[128,2,1024]{2,1,0:T(2,128)(2,1)S(1)}, u32[]{:S(2)}, u32[]{:S(2)}) async-start(bf16[128,2,1024]{2,1,0:T(2,128)(2,1)} %reshape.110), calls=%async_computation.1 | async-start | bytes 1048576 | tf_op jit(solution)/shard_map/all_to_all | solution.py:82
  56.3 45.3 %copy-start.4 = (s32[128,1]{0,1:T(1,128)S(1)}, s32[128,1]{0,1:T(1,128)}, u32[]{:S(2)}) copy-start(s32[128,1]{0,1:T(1,128)} %param.13) | copy-start | bytes 1540
  56.6 56.0 %copy-start.3 = (bf16[1024]{0:T(1024)(128)(2,1)S(1)}, bf16[1024]{0:T(1024)(128)(2,1)}, u32[]{:S(2)}) copy-start(bf16[1024]{0:T(1024)(128)(2,1)} %param.19) | copy-start | bytes 6148
  91.3 42.7 %all-to-all-start.2 = ((bf16[128,2,1024]{2,1,0:T(2,128)(2,1)}), bf16[128,2,1024]{2,1,0:T(2,128)(2,1)S(1)}, u32[]{:S(2)}, u32[]{:S(2)}) async-start(bf16[128,2,1024]{2,1,0:T(2,128)(2,1)} %reshape.115), calls=%async_computation.2 | async-start | bytes 1048576 | tf_op jit(solution)/shard_map/all_to_all | solution.py:91
  101.8 23.9 %collective-permute-start = (bf16[128,1024]{1,0:T(8,128)(2,1)S(1)}, bf16[128,1024]{1,0:T(8,128)(2,1)S(1)}, u32[]{:S(2)}, u32[]{:S(2)}) collective-permute-start(bf16[128,1024]{1,0:T(8,128)(2,1)S(1)} %convolution_convert_fusion.3), channel_id=1, source_target_pairs={{0,1},{1,2},{2,3},{3,0},{4,5},{5,6},{6,7},{7,4},{8,9},{9,10},{10,1... | collective-permute-start | bytes 786440 | tf_op jit(solution)/shard_map/ppermute | solution.py:106
  105.0 20.7 %collective-permute-start.1 = (bf16[128,1024]{1,0:T(8,128)(2,1)S(1)}, bf16[128,1024]{1,0:T(8,128)(2,1)S(1)}, u32[]{:S(2)}, u32[]{:S(2)}) collective-permute-start(bf16[128,1024]{1,0:T(8,128)(2,1)S(1)} %convolution_convert_fusion.3), channel_id=1, source_target_pairs={{0,2},{1,3},{2,0},{3,1},{4,6},{5,7},{6,4},{7,5},{8,10},{9,11},{10,... | collective-permute-start | bytes 786440 | tf_op jit(solution)/shard_map/ppermute | solution.py:106
  109.4 16.3 %collective-permute-start.2 = (bf16[128,1024]{1,0:T(8,128)(2,1)S(1)}, bf16[128,1024]{1,0:T(8,128)(2,1)S(1)}, u32[]{:S(2)}, u32[]{:S(2)}) collective-permute-start(bf16[128,1024]{1,0:T(8,128)(2,1)S(1)} %convolution_convert_fusion.3), channel_id=1, source_target_pairs={{0,3},{1,0},{2,1},{3,2},{4,7},{5,4},{6,5},{7,6},{8,11},{9,8},{10,9... | collective-permute-start | bytes 786440 | tf_op jit(solution)/shard_map/ppermute | solution.py:106
  125.9 8.4 %copy-start.1 = (bf16[256,1024]{1,0:T(8,128)(2,1)S(1)}, bf16[256,1024]{1,0:T(8,128)(2,1)}, u32[]{:S(2)}) copy-start(bf16[256,1024]{1,0:T(8,128)(2,1)} %param.16) | copy-start | bytes 1572868
  125.9 8.4 %copy-start.2 = (bf16[256,1024]{1,0:T(8,128)(2,1)S(1)}, bf16[256,1024]{1,0:T(8,128)(2,1)}, u32[]{:S(2)}) copy-start(bf16[256,1024]{1,0:T(8,128)(2,1)} %param.15) | copy-start | bytes 1572868
Sparse Core Ops, SparseCore 0:
  11.7 169.7 all-gather.1
where the time goes:
time: 197 us; the launch traced here: 196 us
  waiting for transfers between devices  101 us (51%)
  starting transfers between devices  46.2 us (23%)
  between operations  15.1 us (8%)
  blocking collectives  13 us (7%)
  matrix products  10.8 us (5%)
  other arithmetic  5.29 us (3%)
  local copies, waits for them, and re-layouts  4.84 us (2%)
    all_gather x1, waiting for transfers between devices, local(): lax.all_gather(jnp.concatenate([w_query, w_key, w_value], axis=1), 'dp',...  45.6 us
    all_to_all x1, waiting for transfers between devices, local(): lax.all_to_all(pick(wanted, table).astype(jnp.bfloat16).reshape(peers, ca...  33.6 us
    all_to_all x1, starting transfers between devices, local(): lax.all_to_all(requests, 'dp', split_axis=0, concat_axis=0, tiled=True)  20.4 us
    all_to_all x1, waiting for transfers between devices, local(): lax.all_to_all(requests, 'dp', split_axis=0, concat_axis=0, tiled=True)  14.1 us
    all_gather x1, blocking collectives, local(): lax.all_gather(norm_gain, 'mp', axis=0, tiled=True).astype(jnp.float32)  13 us
    ppermute x3, starting transfers between devices, local(): lax.ppermute(joined, 'mp', [(i, (i + k) % parts) for i in range(parts)])  10.6 us
    all_to_all x1, starting transfers between devices, local(): lax.all_to_all(grad_buffer.reshape(peers, capacity, col_width), 'dp', spl...  9.53 us
    all_to_all x1, waiting for transfers between devices, local(): lax.all_to_all(grad_buffer.reshape(peers, capacity, col_width), 'dp', spl...  7.74 us
  transfers between devices with their start and end apart: 7, of which 4 were waited for; matrix products, arithmetic and copies ran while one was open for 6% of the time, Pallas kernels for 0%

commit v1 on v0

--- a/solution.py
+++ b/solution.py
@@ -6,6 +6,12 @@
 
 HD = 128
 SLOT = 128
+
+
+def tiled_gather(x, axis, dim):
+    devices = lax.axis_size(axis)
+    repeats = [devices if d == dim else 1 for d in range(x.ndim)]
+    return lax.all_to_all(jnp.tile(x, repeats), axis, split_axis=dim, concat_axis=dim, tiled=True)
 
 
 def one_hot(rows, columns):
@@ -115,7 +121,7 @@
         ],
         axis=1,
     ).astype(jnp.float32)
-    gain = lax.all_gather(norm_gain, "mp", axis=0, tiled=True).astype(jnp.float32)
+    gain = tiled_gather(norm_gain, "mp", 0).astype(jnp.float32)
     scale = lax.rsqrt(jnp.mean(features * features, axis=1, keepdims=True) + 1e-06)
     normed = (features * scale * gain[None, :]).astype(jnp.bfloat16)
     projected = jnp.dot(normed, weights, preferred_element_type=jnp.float32).astype(jnp.bfloat16)

time: 197 us -> 203 us (1.030)
  waiting for transfers between devices: 101 us -> 116 us
  blocking collectives: 13 us -> 0 us
  starting transfers between devices: 46.2 us -> 49.4 us
    all_gather x1 -> x0, blocking collectives: 13 us -> none  [local(): lax.all_gather(norm_gain, 'mp', axis=0, tiled=True).astype(jnp.float32)]
    ppermute x3, waiting for transfers between devices: 0.01 us -> 9.35 us  [local(): lax.ppermute(joined, 'mp', [(i, (i + k) % parts) for i in range(parts)])]
    all_to_all x1, waiting for transfers between devices: 7.74 us -> 17 us  [local(): lax.all_to_all(grad_buffer.reshape(peers, capacity, col_width), 'dp', spl...]
    all_gather x1, waiting for transfers between devices: 45.6 us -> 39.7 us  [local(): lax.all_gather(jnp.concatenate([w_query, w_key, w_value], axis=1), 'dp',...]
    all_to_all x0 -> x1, starting transfers between devices: none -> 3.96 us  [tiled_gather(): lax.all_to_all(jnp.tile(x, repeats), axis, split_axis=dim, concat_axis=di...]
    all_to_all x0 -> x1, waiting for transfers between devices: none -> 2.67 us  [tiled_gather(): lax.all_to_all(jnp.tile(x, repeats), axis, split_axis=dim, concat_axis=di...]
  transfers between devices with their start and end apart: 7 -> 8, of which waited for: 4 -> 8; matrix products, arithmetic and copies ran while one was open for 6% -> 7% of each run, Pallas kernels for 0% -> 0%
where the time goes in v1:
time: 203 us
  waiting for transfers between devices  116 us (57%)
  starting transfers between devices  49.4 us (24%)
  between operations  15 us (7%)
  matrix products  10.8 us (5%)
  other arithmetic  5.99 us (3%)
  local copies, waits for them, and re-layouts  5.98 us (3%)
    all_gather x1, waiting for transfers between devices, local(): lax.all_gather(jnp.concatenate([w_query, w_key, w_value], axis=1), 'dp',...  39.7 us
    all_to_all x1, waiting for transfers between devices, local(): lax.all_to_all(pick(wanted, table).astype(jnp.bfloat16).reshape(peers, ca...  32.7 us
    all_to_all x1, starting transfers between devices, local(): lax.all_to_all(requests, 'dp', split_axis=0, concat_axis=0, tiled=True)  20.4 us
    all_to_all x1, waiting for transfers between devices, local(): lax.all_to_all(grad_buffer.reshape(peers, capacity, col_width), 'dp', spl...  17 us
    all_to_all x1, waiting for transfers between devices, local(): lax.all_to_all(requests, 'dp', split_axis=0, concat_axis=0, tiled=True)  14.1 us
    all_to_all x1, starting transfers between devices, local(): lax.all_to_all(grad_buffer.reshape(peers, capacity, col_width), 'dp', spl...  10.5 us
    ppermute x3, waiting for transfers between devices, local(): lax.ppermute(joined, 'mp', [(i, (i + k) % parts) for i in range(parts)])  9.35 us
    ppermute x3, starting transfers between devices, local(): lax.ppermute(joined, 'mp', [(i, (i + k) % parts) for i in range(parts)])  8.84 us
  transfers between devices with their start and end apart: 8, of which 8 were waited for; matrix products, arithmetic and copies ran while one was open for 7% of the time, Pallas kernels for 0%

profile of v1, /device:TPU:1, one launch (start us, length us, event | category | flops | bytes accessed | tf_op | source)
XLA Modules:
  0.0 202.8 jit_solution(12761054761555591407)
XLA Ops:
  7.2 0.0 copy-start
  7.2 0.0 all-gather.2.cloned.1.call-start
  7.2 1.5 pad_maximum_fusion.3
  8.7 0.0 all-gather.2.cloned.1.call-update
  8.7 0.9 convert_reduce_fusion
  9.6 0.7 multiply_add_fusion
  10.3 0.1 select_reduce_fusion
  10.4 0.0 copy-start.3
  10.4 0.8 sub.24
  11.2 20.4 %all-to-all-start = ((s32[128,1,2]{2,1,0:T(1,128)}), s32[128,1,2]{2,1,0:T(1,128)S(1)}, u32[]{:S(2)}, u32[]{:S(2)}) async-start(s32[128,1,2]{2,1,0:T(1,128)} %bitcast.4), calls=%async_computation | async-start | bytes 131072 | tf_op jit(solution)/shard_map/all_to_all | solution.py:81
  31.6 0.7 convert_element_type.62
  32.3 14.1 %all-to-all-done = s32[128,1,2]{2,1,0:T(1,128)S(1)} async-done(((s32[128,1,2]{2,1,0:T(1,128)}), s32[128,1,2]{2,1,0:T(1,128)S(1)}, u32[]{:S(2)}, u32[]{:S(2)}) %all-to-all-start) | async-done | bytes 1056 | tf_op jit(solution)/shard_map/all_to_all | solution.py:81
  46.4 0.5 broadcast.76
  47.0 0.8 reduce.3
  47.8 0.1 eq.74
  47.9 1.6 convolution_convert_fusion.1
  49.6 1.0 reshape.120
  50.6 5.7 %all-to-all-start.1 = ((bf16[128,2,1024]{2,1,0:T(2,128)(2,1)}), bf16[128,2,1024]{2,1,0:T(2,128)(2,1)S(1)}, u32[]{:S(2)}, u32[]{:S(2)}) async-start(bf16[128,2,1024]{2,1,0:T(2,128)(2,1)} %reshape.120), calls=%async_computation.1 | async-start | bytes 1048576 | tf_op jit(solution)/shard_map/all_to_all | solution.py:88
  56.3 0.0 copy-done.3
  56.3 0.0 copy-start.4
  56.3 0.5 broadcast.77
  56.8 0.7 reduce.4
  57.5 0.6 reshape.137
  58.1 32.7 %all-to-all-done.1 = bf16[128,2,1024]{2,1,0:T(2,128)(2,1)S(1)} async-done(((bf16[128,2,1024]{2,1,0:T(2,128)(2,1)}), bf16[128,2,1024]{2,1,0:T(2,128)(2,1)S(1)}, u32[]{:S(2)}, u32[]{:S(2)}) %all-to-all-start.1) | async-done | bytes 524320 | tf_op jit(solution)/shard_map/all_to_all | solution.py:88
  90.8 4.0 %all-to-all-start.2 = ((bf16[4,2,512]{2,1,0:T(2,128)(2,1)}), bf16[4,2,512]{2,1,0:T(2,128)(2,1)S(1)}, u32[]{:S(2)}, u32[]{:S(2)}) async-start(bf16[4,2,512]{2,1,0:T(2,128)(2,1)} %reshape.137), calls=%async_computation.2 | async-start | bytes 16384 | tf_op jit(solution)/shard_map/all_to_all | solution.py:14
  94.8 0.0 copy-done
  94.8 0.3 convolution_convert_fusion.2
  95.1 0.2 reshape.121
  95.3 1.0 reshape.125
  96.3 2.7 %all-to-all-done.2 = bf16[4,2,512]{2,1,0:T(2,128)(2,1)S(1)} async-done(((bf16[4,2,512]{2,1,0:T(2,128)(2,1)}), bf16[4,2,512]{2,1,0:T(2,128)(2,1)S(1)}, u32[]{:S(2)}, u32[]{:S(2)}) %all-to-all-start.2) | async-done | bytes 8224 | tf_op jit(solution)/shard_map/all_to_all | solution.py:14
  98.9 10.5 %all-to-all-start.3 = ((bf16[128,2,1024]{2,1,0:T(2,128)(2,1)}), bf16[128,2,1024]{2,1,0:T(2,128)(2,1)S(1)}, u32[]{:S(2)}, u32[]{:S(2)}) async-start(bf16[128,2,1024]{2,1,0:T(2,128)(2,1)} %reshape.125), calls=%async_computation.3 | async-start | bytes 1048576 | tf_op jit(solution)/shard_map/all_to_all | solution.py:97
  110.1 0.0 copy-done.4
  110.1 0.3 convolution_convert_fusion.3
  110.4 2.2 %collective-permute-start = (bf16[128,1024]{1,0:T(8,128)(2,1)S(1)}, bf16[128,1024]{1,0:T(8,128)(2,1)S(1)}, u32[]{:S(2)}, u32[]{:S(2)}) collective-permute-start(bf16[128,1024]{1,0:T(8,128)(2,1)S(1)} %convolution_convert_fusion.3), channel_id=1, source_target_pairs={{0,1},{1,2},{2,3},{3,0},{4,5},{5,6},{6,7},{7,4},{8,9},{9,10},{10,1... | collective-permute-start | bytes 786440 | tf_op jit(solution)/shard_map/ppermute | solution.py:112
  112.6 3.7 %collective-permute-start.1 = (bf16[128,1024]{1,0:T(8,128)(2,1)S(1)}, bf16[128,1024]{1,0:T(8,128)(2,1)S(1)}, u32[]{:S(2)}, u32[]{:S(2)}) collective-permute-start(bf16[128,1024]{1,0:T(8,128)(2,1)S(1)} %convolution_convert_fusion.3), channel_id=1, source_target_pairs={{0,2},{1,3},{2,0},{3,1},{4,6},{5,7},{6,4},{7,5},{8,10},{9,11},{10,... | collective-permute-start | bytes 786440 | tf_op jit(solution)/shard_map/ppermute | solution.py:112
  116.3 3.0 %collective-permute-start.2 = (bf16[128,1024]{1,0:T(8,128)(2,1)S(1)}, bf16[128,1024]{1,0:T(8,128)(2,1)S(1)}, u32[]{:S(2)}, u32[]{:S(2)}) collective-permute-start(bf16[128,1024]{1,0:T(8,128)(2,1)S(1)} %convolution_convert_fusion.3), channel_id=1, source_target_pairs={{0,3},{1,0},{2,1},{3,2},{4,7},{5,4},{6,5},{7,6},{8,11},{9,8},{10,9... | collective-permute-start | bytes 786440 | tf_op jit(solution)/shard_map/ppermute | solution.py:112
  119.3 0.1 fusion.27
  119.5 1.6 collective-permute-done
  121.1 4.4 %collective-permute-done.1 = bf16[128,1024]{1,0:T(8,128)(2,1)S(1)} collective-permute-done((bf16[128,1024]{1,0:T(8,128)(2,1)S(1)}, bf16[128,1024]{1,0:T(8,128)(2,1)S(1)}, u32[]{:S(2)}, u32[]{:S(2)}) %collective-permute-start.1) | collective-permute-done | bytes 262176 | tf_op jit(solution)/shard_map/ppermute | solution.py:112
  125.5 3.3 %collective-permute-done.2 = bf16[128,1024]{1,0:T(8,128)(2,1)S(1)} collective-permute-done((bf16[128,1024]{1,0:T(8,128)(2,1)S(1)}, bf16[128,1024]{1,0:T(8,128)(2,1)S(1)}, u32[]{:S(2)}, u32[]{:S(2)}) %collective-permute-start.2) | collective-permute-done | bytes 262176 | tf_op jit(solution)/shard_map/ppermute | solution.py:112
  128.8 0.1 pad_maximum_fusion
  128.9 0.0 copy-start.1
  129.0 0.0 copy-start.2
  129.0 0.1 dynamic-slice_bitcast_fusion.3
  129.1 0.3 fusion.1
  129.4 17.0 %all-to-all-done.3 = bf16[128,2,1024]{2,1,0:T(2,128)(2,1)S(1)} async-done(((bf16[128,2,1024]{2,1,0:T(2,128)(2,1)}), bf16[128,2,1024]{2,1,0:T(2,128)(2,1)S(1)}, u32[]{:S(2)}, u32[]{:S(2)}) %all-to-all-start.3) | async-done | bytes 524320 | tf_op jit(solution)/shard_map/all_to_all | solution.py:97
  146.4 0.2 reshape.126
  146.6 0.0 copy-done.1
  146.6 0.0 copy-done.2
  146.6 1.7 convert_multiply_fusion.4
  148.4 39.7 %all-gather.2.cloned.1.call-done = bf16[4096,1536]{1,0:T(8,128)(2,1)} async-done(((bf16[32,1536]{1,0:T(8,128)(2,1)}), bf16[4096,1536]{1,0:T(8,128)(2,1)}) %all-gather.2.cloned.1.call-update) | async-done | bytes 12582928 | tf_op jit(solution)/shard_map/all_gather | solution.py:70
  188.1 6.4 %convolution_convert_fusion = bf16[128,1536]{1,0:T(8,128)(2,1)S(1)} fusion(bf16[4096,1536]{1,0:T(8,128)(2,1)} %all-gather.2.cloned.1.call-done, f32[4096]{0:T(1024)S(1)} %bitcast.55, f32[128]{0:T(128)S(1)} %add_rsqrt_fusion, bf16[128,1024]{1,0:T(8,128)(2,1)S(1)} %get-tuple-element.22, bf16[128,1024]{1,0:T(8,128)(2,1)S(1)} %get-tuple-element.23, ...), kind=kOutput, calls=%fused_computation.3 | convolution fusion | flops 1616576512 | bytes 14041600 | tf_op jit(solution)/shard_map/dot_general | solution.py:127
  194.5 0.2 fusion.5
  194.8 0.1 fusion.31
  194.9 0.1 copy.38
  195.0 0.2 fusion.7
  195.2 0.8 copy.36
  (8 shorter events, 0.1 us)
Async XLA Ops:
  7.2 87.6 %copy-start = (bf16[128,1024]{1,0:T(8,128)(2,1)S(1)}, bf16[128,1024]{1,0:T(8,128)(2,1)}, u32[]{:S(2)}) copy-start(bf16[128,1024]{1,0:T(8,128)(2,1)} %param.23) | copy-start | bytes 786436
  7.2 180.9 %all-gather.2.cloned.1.call-start = ((), (), s32[]{:S(2)}) async-start(), calls=%async_computation.4 | async-start | bytes 12681216 | tf_op jit(solution)/shard_map/all_gather | solution.py:70
  10.4 45.8 %copy-start.3 = (bf16[1024]{0:T(1024)(128)(2,1)S(1)}, bf16[1024]{0:T(1024)(128)(2,1)}, u32[]{:S(2)}) copy-start(bf16[1024]{0:T(1024)(128)(2,1)} %param.19) | copy-start | bytes 6148
  11.2 35.2 %all-to-all-start = ((s32[128,1,2]{2,1,0:T(1,128)}), s32[128,1,2]{2,1,0:T(1,128)S(1)}, u32[]{:S(2)}, u32[]{:S(2)}) async-start(s32[128,1,2]{2,1,0:T(1,128)} %bitcast.4), calls=%async_computation | async-start | bytes 131072 | tf_op jit(solution)/shard_map/all_to_all | solution.py:81
  50.6 40.2 %all-to-all-start.1 = ((bf16[128,2,1024]{2,1,0:T(2,128)(2,1)}), bf16[128,2,1024]{2,1,0:T(2,128)(2,1)S(1)}, u32[]{:S(2)}, u32[]{:S(2)}) async-start(bf16[128,2,1024]{2,1,0:T(2,128)(2,1)} %reshape.120), calls=%async_computation.1 | async-start | bytes 1048576 | tf_op jit(solution)/shard_map/all_to_all | solution.py:88
  56.3 53.8 %copy-start.4 = (s32[128,1]{0,1:T(1,128)S(1)}, s32[128,1]{0,1:T(1,128)}, u32[]{:S(2)}) copy-start(s32[128,1]{0,1:T(1,128)} %param.13) | copy-start | bytes 1540
  90.8 8.1 %all-to-all-start.2 = ((bf16[4,2,512]{2,1,0:T(2,128)(2,1)}), bf16[4,2,512]{2,1,0:T(2,128)(2,1)S(1)}, u32[]{:S(2)}, u32[]{:S(2)}) async-start(bf16[4,2,512]{2,1,0:T(2,128)(2,1)} %reshape.137), calls=%async_computation.2 | async-start | bytes 16384 | tf_op jit(solution)/shard_map/all_to_all | solution.py:14
  98.9 47.5 %all-to-all-start.3 = ((bf16[128,2,1024]{2,1,0:T(2,128)(2,1)}), bf16[128,2,1024]{2,1,0:T(2,128)(2,1)S(1)}, u32[]{:S(2)}, u32[]{:S(2)}) async-start(bf16[128,2,1024]{2,1,0:T(2,128)(2,1)} %reshape.125), calls=%async_computation.3 | async-start | bytes 1048576 | tf_op jit(solution)/shard_map/all_to_all | solution.py:97
  110.4 10.7 %collective-permute-start = (bf16[128,1024]{1,0:T(8,128)(2,1)S(1)}, bf16[128,1024]{1,0:T(8,128)(2,1)S(1)}, u32[]{:S(2)}, u32[]{:S(2)}) collective-permute-start(bf16[128,1024]{1,0:T(8,128)(2,1)S(1)} %convolution_convert_fusion.3), channel_id=1, source_target_pairs={{0,1},{1,2},{2,3},{3,0},{4,5},{5,6},{6,7},{7,4},{8,9},{9,10},{10,1... | collective-permute-start | bytes 786440 | tf_op jit(solution)/shard_map/ppermute | solution.py:112
  112.6 12.9 %collective-permute-start.1 = (bf16[128,1024]{1,0:T(8,128)(2,1)S(1)}, bf16[128,1024]{1,0:T(8,128)(2,1)S(1)}, u32[]{:S(2)}, u32[]{:S(2)}) collective-permute-start(bf16[128,1024]{1,0:T(8,128)(2,1)S(1)} %convolution_convert_fusion.3), channel_id=1, source_target_pairs={{0,2},{1,3},{2,0},{3,1},{4,6},{5,7},{6,4},{7,5},{8,10},{9,11},{10,... | collective-permute-start | bytes 786440 | tf_op jit(solution)/shard_map/ppermute | solution.py:112
  116.3 12.5 %collective-permute-start.2 = (bf16[128,1024]{1,0:T(8,128)(2,1)S(1)}, bf16[128,1024]{1,0:T(8,128)(2,1)S(1)}, u32[]{:S(2)}, u32[]{:S(2)}) collective-permute-start(bf16[128,1024]{1,0:T(8,128)(2,1)S(1)} %convolution_convert_fusion.3), channel_id=1, source_target_pairs={{0,3},{1,0},{2,1},{3,2},{4,7},{5,4},{6,5},{7,6},{8,11},{9,8},{10,9... | collective-permute-start | bytes 786440 | tf_op jit(solution)/shard_map/ppermute | solution.py:112
  128.9 17.7 %copy-start.1 = (bf16[256,1024]{1,0:T(8,128)(2,1)S(1)}, bf16[256,1024]{1,0:T(8,128)(2,1)}, u32[]{:S(2)}) copy-start(bf16[256,1024]{1,0:T(8,128)(2,1)} %param.16) | copy-start | bytes 1572868
  129.0 17.7 %copy-start.2 = (bf16[256,1024]{1,0:T(8,128)(2,1)S(1)}, bf16[256,1024]{1,0:T(8,128)(2,1)}, u32[]{:S(2)}) copy-start(bf16[256,1024]{1,0:T(8,128)(2,1)} %param.15) | copy-start | bytes 1572868
Sparse Core Ops, SparseCore 0:
  11.7 176.3 all-gather.1
